TPU v7x, 32 devices: a whole 2x2x4 slice. The times are simulated.
32 devices in a mesh: groups: 2 (over y), tm: 4 (over x, core), space: 4 (over z).
Axes of the slice: x: 2, y: 2, z: 4, core: 2. Of those that a mesh axis runs over, the one named last changes fastest.
Arguments:
- features: bfloat16 [8, 32, 128, 256], P(('groups', 'tm'), 'space'), parts along dimension 0, may hold values from -6 to 6
- pair_order: int32 [8], P(('groups', 'tm')), parts along dimension 0, may hold values 0 or 1
- flow_now: bfloat16 [8, 2, 32, 128], P(('groups', 'tm'), None, 'space'), parts along dimension 0, may hold values from -8 to 8
- targets: int32 [8, 2, 32, 128], P(('groups', 'tm'), None, 'space'), parts along dimension 0, may hold values from -4 to 4
- w_volume: bfloat16 [162, 128], replicated, may hold values from -0.5 to 0.5
- b_volume: float32 [128], replicated, may hold values from -3 to 3
- w_code: bfloat16 [3, 3, 128, 128], replicated, may hold values from -0.1875 to 0.1875
- b_code: float32 [128], replicated, may hold values from -3 to 3
- w_flow: bfloat16 [7, 7, 2, 128], replicated, may hold values from -0.625 to 0.625
- b_flow: float32 [128], replicated, may hold values from -3 to 3
- w_joint: bfloat16 [3, 3, 256, 128], replicated, may hold values from -0.125 to 0.125
- b_joint: float32 [128], replicated, may hold values from -3 to 3
- w_head: bfloat16 [128, 2], replicated, may hold values from -0.5 to 0.5
- b_head: float32 [2], replicated, may hold values from -3 to 3
Outputs:
- loss: float32 [2], P('groups'), parts along dimension 0
- flow_error: float32 [8, 2, 32, 128], P(('groups', 'tm'), None, 'space'), parts along dimension 0
- grad_w_volume: float32 [324, 128], P('groups'), parts along dimension 0
- grad_b_volume: float32 [256], P('groups'), parts along dimension 0
- grad_w_code: float32 [6, 3, 128, 128], P('groups'), parts along dimension 0
- grad_b_code: float32 [256], P('groups'), parts along dimension 0
- grad_w_flow: float32 [14, 7, 2, 128], P('groups'), parts along dimension 0
- grad_b_flow: float32 [256], P('groups'), parts along dimension 0
- grad_w_joint: float32 [6, 3, 256, 128], P('groups'), parts along dimension 0
- grad_b_joint: float32 [256], P('groups'), parts along dimension 0
- grad_w_head: float32 [256, 2], P('groups'), parts along dimension 0
- grad_b_head: float32 [4], P('groups'), parts along dimension 0
There are 2 independent parts, one for each index of `groups`. A program takes and returns all parts, laid end to end along the dimension named above; an argument that names none is the same for every part. Nothing has to cross between parts.
All inputs are finite; a program needn't handle non-finite values. No bound on the sum of `pair_order` on one device may be relied on, other than what follows from the above.
Results may differ from a plain program's by a relative error of at most 0.0032.
Values may be sent and summed in bfloat16 or wider, within the bound.
No kernel may reach another device: no remote copies, remote signals or barrier semaphores. Data moves between devices by JAX's collectives and lax.ppermute only.
A program may use at most 64 MiB of HBM per device.

v0:
```python
import jax
import jax.numpy as jnp
from jax import lax
from jax.sharding import PartitionSpec as P

RADIUS = 4
highest_precision = lax.Precision.HIGHEST


def extended_2(array, sides, width):
    for axis, dim in sides:
        devices, length = (lax.axis_size(axis), array.shape[dim])
        up = [(i, (i + 1) % devices) for i in range(devices - 1)]
        down = [(j, i) for i, j in up]
        last = lax.slice_in_dim(array, length - width, length, axis=dim)
        first = lax.slice_in_dim(array, 0, width, axis=dim)
        before = lax.ppermute(last, axis, up)
        after = lax.ppermute(first, axis, down)
        array = jnp.concatenate([before, array, after], axis=dim)
    return array


def shifted(block, axis, distance):
    devices = range(lax.axis_size(axis))
    route = [(i - distance, i) for i in devices if i - distance in devices]
    return lax.ppermute(block, axis, route)


def silu_slope(values):
    sigma = jax.nn.sigmoid(values)
    return sigma * (1.0 + values * (1.0 - sigma))


def correlate(own_tile, other_ext):
    n_rows = own_tile.shape[0]
    n_cols = own_tile.shape[1]
    n_chan = own_tile.shape[2]
    side = 2 * RADIUS + 1
    padded_other = jnp.pad(other_ext, ((0, 0), (RADIUS, RADIUS), (0, 0)))
    bands = []
    for row_off in range(side):
        window = padded_other[row_off : row_off + n_rows]
        scores = jnp.einsum("rxc,ryc->rxy", own_tile, window, preferred_element_type=jnp.float32)
        flat_scores = scores.reshape(n_rows, n_cols * (n_cols + 2 * RADIUS))
        flat_scores = jnp.pad(flat_scores, ((0, 0), (0, n_cols)))
        bands.append(flat_scores.reshape(n_rows, n_cols, n_cols + side)[:, :, :side])
    stacked = jnp.stack(bands, axis=2).reshape(n_rows, n_cols, side * side)
    return (stacked * n_chan ** (-0.5)).astype(jnp.bfloat16)


def column_stack(extended, ksize):
    half_k = ksize // 2
    n_cols = extended.shape[1]
    padded = jnp.pad(extended, ((0, 0), (half_k, half_k), (0, 0)))
    return jnp.concatenate([padded[:, j : j + n_cols] for j in range(ksize)], axis=-1)


def conv_tile(extended, weight):
    ksize = weight.shape[0]
    half_k = ksize // 2
    n_rows = extended.shape[0] - 2 * half_k
    n_cols = extended.shape[1]
    stacked = column_stack(extended, ksize)
    depth = stacked.shape[2]
    summed = jnp.zeros((n_rows * n_cols, weight.shape[3]), jnp.float32)
    for i in range(ksize):
        taken = stacked[i : i + n_rows].reshape(n_rows * n_cols, depth)
        summed = summed + jnp.dot(
            taken, weight[i].reshape(depth, weight.shape[3]), preferred_element_type=jnp.float32
        )
    return summed


def conv_tile_back(extended_slope, weight):
    ksize = weight.shape[0]
    half_k = ksize // 2
    n_rows = extended_slope.shape[0] - 2 * half_k
    n_cols = extended_slope.shape[1]
    stacked = column_stack(extended_slope, ksize)
    depth = stacked.shape[2]
    summed = jnp.zeros((n_rows * n_cols, weight.shape[2]), jnp.float32)
    for row_at in range(ksize):
        i = ksize - 1 - row_at
        taken = stacked[row_at : row_at + n_rows].reshape(n_rows * n_cols, depth)
        w_rows = jnp.concatenate([weight[i, ksize - 1 - col_at] for col_at in range(ksize)], axis=1)
        summed = summed + lax.dot_general(
            taken, w_rows, (((1,), (1,)), ((), ())), preferred_element_type=jnp.float32
        )
    return summed


def conv_tile_grad(extended, slope_flat, ksize):
    half_k = ksize // 2
    n_rows = extended.shape[0] - 2 * half_k
    n_cols = extended.shape[1]
    stacked = column_stack(extended, ksize)
    depth = stacked.shape[2]
    taps = []
    for i in range(ksize):
        taken = stacked[i : i + n_rows].reshape(n_rows * n_cols, depth)
        rows_grad = lax.dot_general(
            taken, slope_flat, (((0,), (0,)), ((), ())), preferred_element_type=jnp.float32
        )
        taps.append(rows_grad.reshape(ksize, extended.shape[2], slope_flat.shape[1]))
    return jnp.stack(taps, axis=0)


def local(
    features,
    pair_order,
    flow_now,
    targets,
    w_volume,
    b_volume,
    w_code,
    b_code,
    w_flow,
    b_flow,
    w_joint,
    b_joint,
    w_head,
    b_head,
):
    own_tile = features[0]
    n_rows = own_tile.shape[0]
    n_cols = own_tile.shape[1]
    n_pix = n_rows * n_cols
    n_code = w_code.shape[3]
    own_ext = extended_2(own_tile, (("space", 0),), RADIUS)
    next_ext = shifted(own_ext, "tm", -1)
    forward = correlate(own_tile, next_ext)
    prior_ext = shifted(own_ext, "tm", 1)
    backward = correlate(own_tile, prior_ext)
    swapped = pair_order[0] == 1
    first_half = jnp.where(swapped, backward, forward)
    second_half = jnp.where(swapped, forward, backward)
    volume = jnp.concatenate([first_half, second_half], axis=-1)
    volume_flat = volume.reshape(n_pix, volume.shape[2])
    code_pre = jnp.dot(volume_flat, w_volume, preferred_element_type=jnp.float32) + b_volume
    code = jax.nn.silu(code_pre).astype(jnp.bfloat16)
    code_ext = extended_2(code.reshape(n_rows, n_cols, n_code), (("space", 0),), 1)
    motion_pre = conv_tile(code_ext, w_code) + b_code
    motion = jax.nn.silu(motion_pre).astype(jnp.bfloat16)
    flow_ext = extended_2(flow_now[0], (("space", 1),), 3)
    padded_flow = jnp.pad(flow_ext, ((0, 0), (0, 0), (3, 3)))
    patch_list = []
    for i in range(7):
        for j in range(7):
            for comp in range(2):
                patch_list.append(padded_flow[comp, i : i + n_rows, j : j + n_cols].reshape(n_pix))
    patches = jnp.stack(patch_list, axis=0)
    flow_weight = w_flow.reshape(98, n_code)
    flow_pre = (
        lax.dot_general(
            patches, flow_weight, (((0,), (0,)), ((), ())), preferred_element_type=jnp.float32
        )
        + b_flow
    )
    flow_code = jax.nn.silu(flow_pre).astype(jnp.bfloat16)
    joint = jnp.concatenate([motion, flow_code], axis=-1)
    joint_ext = extended_2(joint.reshape(n_rows, n_cols, 2 * n_code), (("space", 0),), 1)
    hidden_pre = conv_tile(joint_ext, w_joint) + b_joint
    hidden = jax.nn.silu(hidden_pre).astype(jnp.bfloat16)
    pred = jnp.dot(hidden, w_head, preferred_element_type=jnp.float32) + b_head
    target_flat = targets[0].reshape(2, n_pix).T.astype(jnp.float32)
    error_flat = pred - target_flat
    flow_error = error_flat.T.reshape(1, 2, n_rows, n_cols)
    n_frames = lax.axis_size("tm")
    frame_at = lax.axis_index("tm").astype(jnp.float32)
    frame_weight = jnp.power(jnp.float32(0.25), (n_frames - 1 - frame_at) / (n_frames - 1))
    count = 2.0 * n_frames * n_rows * lax.axis_size("space") * n_cols
    loss_local = jnp.reshape(frame_weight * jnp.sum(error_flat * error_flat) / count, (1,))
    slope_pred = 2.0 * frame_weight * error_flat / count
    grad_w_head = jnp.dot(hidden.astype(jnp.float32).T, slope_pred, precision=highest_precision)
    grad_b_head = jnp.sum(slope_pred, axis=0)
    slope_hidden = (
        jnp.dot(slope_pred, w_head.astype(jnp.float32).T, precision=highest_precision)
        * silu_slope(hidden_pre)
    ).astype(jnp.bfloat16)
    grad_w_joint = conv_tile_grad(joint_ext, slope_hidden, 3)
    grad_b_joint = jnp.sum(slope_hidden.astype(jnp.float32), axis=0)
    slope_ext = extended_2(slope_hidden.reshape(n_rows, n_cols, n_code), (("space", 0),), 1)
    slope_joint = conv_tile_back(slope_ext, w_joint)
    slope_motion = (slope_joint[:, :n_code] * silu_slope(motion_pre)).astype(jnp.bfloat16)
    slope_flow = (slope_joint[:, n_code:] * silu_slope(flow_pre)).astype(jnp.bfloat16)
    grad_w_flow = jnp.dot(patches, slope_flow, preferred_element_type=jnp.float32).reshape(
        7, 7, 2, n_code
    )
    grad_b_flow = jnp.sum(slope_flow.astype(jnp.float32), axis=0)
    grad_w_code = conv_tile_grad(code_ext, slope_motion, 3)
    grad_b_code = jnp.sum(slope_motion.astype(jnp.float32), axis=0)
    motion_ext = extended_2(slope_motion.reshape(n_rows, n_cols, n_code), (("space", 0),), 1)
    slope_code = (conv_tile_back(motion_ext, w_code) * silu_slope(code_pre)).astype(jnp.bfloat16)
    grad_w_volume = lax.dot_general(
        volume_flat, slope_code, (((0,), (0,)), ((), ())), preferred_element_type=jnp.float32
    )
    grad_b_volume = jnp.sum(slope_code.astype(jnp.float32), axis=0)
    (
        loss_local,
        grad_w_volume,
        grad_b_volume,
        grad_w_code,
        grad_b_code,
        grad_w_flow,
        grad_b_flow,
        grad_w_joint,
        grad_b_joint,
        grad_w_head,
        grad_b_head,
    ) = lax.psum(
        (
            loss_local,
            grad_w_volume,
            grad_b_volume,
            grad_w_code,
            grad_b_code,
            grad_w_flow,
            grad_b_flow,
            grad_w_joint,
            grad_b_joint,
            grad_w_head,
            grad_b_head,
        ),
        ("tm", "space"),
    )
    return (
        loss_local,
        flow_error,
        grad_w_volume,
        grad_b_volume,
        grad_w_code,
        grad_b_code,
        grad_w_flow,
        grad_b_flow,
        grad_w_joint,
        grad_b_joint,
        grad_w_head,
        grad_b_head,
    )


def solution(mesh):
    placed = (
        P(("groups", "tm"), "space", None, None),
        P(("groups", "tm")),
        P(("groups", "tm"), None, "space", None),
        P(("groups", "tm"), None, "space", None),
        P(),
        P(),
        P(),
        P(),
        P(),
        P(),
        P(),
        P(),
        P(),
        P(),
    )
    return jax.shard_map(
        local,
        mesh=mesh,
        in_specs=placed,
        out_specs=(
            P("groups"),
            P(("groups", "tm"), None, "space", None),
            P("groups", None),
            P("groups"),
            P("groups", None, None, None),
            P("groups"),
            P("groups", None, None, None),
            P("groups"),
            P("groups", None, None, None),
            P("groups"),
            P("groups", None),
            P("groups"),
        ),
        check_vma=False,
    )
```

profile of v0, /device:TPU:0, one launch (start us, length us, event | category | flops | bytes accessed | tf_op | source)
XLA Modules:
  0.0 301.7 jit_solution(11512304857704696042)
XLA Ops:
  8.4 4.9 %collective-permute-start = (bf16[4,128,256]{2,1,0:T(8,128)(2,1)S(1)}, bf16[4,128,256]{2,1,0:T(8,128)(2,1)S(1)}, u32[]{:S(2)}, u32[]{:S(2)}) collective-permute-start(bf16[4,128,256]{2,1,0:T(8,128)(2,1)S(1)} %get-tuple-element.61), channel_id=1, source_target_pairs={{0,1},{1,2},{2,3},{4,5},{5,6},{6,7},{8,9},{9,10},{10,11},{12,13},{... | collective-permute-start | bytes 786440 | tf_op jit(solution)/shard_map/ppermute | solution.py:17
  15.4 4.5 %collective-permute-start.6 = (bf16[2,3,128]{2,1,0:T(4,128)(2,1)S(1)}, bf16[2,3,128]{2,1,0:T(4,128)(2,1)S(1)}, u32[]{:S(2)}, u32[]{:S(2)}) collective-permute-start(bf16[2,3,128]{2,1,0:T(4,128)(2,1)S(1)} %get-tuple-element.186), channel_id=1, source_target_pairs={{0,1},{1,2},{2,3},{4,5},{5,6},{6,7},{8,9},{9,10},{10,11},{12,13},{... | collective-permute-start | bytes 4616 | tf_op jit(solution)/shard_map/ppermute | solution.py:17
  22.0 2.0 fusion.158
  32.2 4.2 %collective-permute-start.2 = (bf16[16,128,256]{2,1,0:T(8,128)(2,1)}, bf16[16,128,256]{2,1,0:T(8,128)(2,1)}, u32[]{:S(2)}, u32[]{:S(2)}) collective-permute-start(bf16[16,128,256]{2,1,0:T(8,128)(2,1)} %pad_maximum_fusion.2), channel_id=1, source_target_pairs={{0,4},{4,8},{8,12},{1,5},{5,9},{9,13},{2,6},{6,10},{10,14},{3,7},{... | collective-permute-start | bytes 3145736 | tf_op jit(solution)/shard_map/ppermute | solution.py:26
  55.9 1.8 convolution_bitcast_fusion.3
  114.4 4.5 %collective-permute-start.4 = (bf16[1,128,128]{2,1,0:T(8,128)(2,1)S(1)}, bf16[1,128,128]{2,1,0:T(8,128)(2,1)S(1)}, u32[]{:S(2)}, u32[]{:S(2)}) collective-permute-start(bf16[1,128,128]{2,1,0:T(8,128)(2,1)S(1)} %get-tuple-element.85), channel_id=1, source_target_pairs={{0,1},{1,2},{2,3},{4,5},{5,6},{6,7},{8,9},{9,10},{10,11},{12,13},{... | collective-permute-start | bytes 98312 | tf_op jit(solution)/shard_map/ppermute | solution.py:17
  121.3 3.4 %collective-permute-done.5 = bf16[1,128,128]{2,1,0:T(8,128)(2,1)S(1)} collective-permute-done((bf16[1,128,128]{2,1,0:T(8,128)(2,1)S(1)}, bf16[1,128,128]{2,1,0:T(8,128)(2,1)S(1)}, u32[]{:S(2)}, u32[]{:S(2)}) %collective-permute-start.5) | collective-permute-done | bytes 32800 | tf_op jit(solution)/shard_map/ppermute | solution.py:18
  132.0 3.5 %collective-permute-start.8 = (bf16[1,128,256]{2,1,0:T(8,128)(2,1)S(1)}, bf16[1,128,256]{2,1,0:T(8,128)(2,1)S(1)}, u32[]{:S(2)}, u32[]{:S(2)}) collective-permute-start(bf16[1,128,256]{2,1,0:T(8,128)(2,1)S(1)} %get-tuple-element.59), channel_id=1, source_target_pairs={{0,1},{1,2},{2,3},{4,5},{5,6},{6,7},{8,9},{9,10},{10,11},{12,13},{... | collective-permute-start | bytes 196616 | tf_op jit(solution)/shard_map/ppermute | solution.py:17
  135.5 1.5 collective-permute-start.9
  137.4 4.3 %collective-permute-done.9 = bf16[1,128,256]{2,1,0:T(8,128)(2,1)S(1)} collective-permute-done((bf16[1,128,256]{2,1,0:T(8,128)(2,1)S(1)}, bf16[1,128,256]{2,1,0:T(8,128)(2,1)S(1)}, u32[]{:S(2)}, u32[]{:S(2)}) %collective-permute-start.9) | collective-permute-done | bytes 65568 | tf_op jit(solution)/shard_map/ppermute | solution.py:18
  142.2 1.7 fusion.153
  143.9 1.6 copy.98
  145.5 2.4 fusion.165
  148.7 2.3 fusion.166
  151.0 1.7 copy.97
  152.7 2.4 multiply_convert_fusion
  159.1 3.5 %collective-permute-start.10 = (bf16[1,128,128]{2,1,0:T(8,128)(2,1)S(1)}, bf16[1,128,128]{2,1,0:T(8,128)(2,1)S(1)}, u32[]{:S(2)}, u32[]{:S(2)}) collective-permute-start(bf16[1,128,128]{2,1,0:T(8,128)(2,1)S(1)} %get-tuple-element.83), channel_id=1, source_target_pairs={{0,1},{1,2},{2,3},{4,5},{5,6},{6,7},{8,9},{9,10},{10,11},{12,13},{... | collective-permute-start | bytes 98312 | tf_op jit(solution)/shard_map/ppermute | solution.py:17
  165.0 3.4 %collective-permute-done.11 = bf16[1,128,128]{2,1,0:T(8,128)(2,1)S(1)} collective-permute-done((bf16[1,128,128]{2,1,0:T(8,128)(2,1)S(1)}, bf16[1,128,128]{2,1,0:T(8,128)(2,1)S(1)}, u32[]{:S(2)}, u32[]{:S(2)}) %collective-permute-start.11) | collective-permute-done | bytes 32800 | tf_op jit(solution)/shard_map/ppermute | solution.py:18
  174.0 1.9 collective-permute-start.12
  178.1 3.6 %collective-permute-done.13 = bf16[1,128,128]{2,1,0:T(8,128)(2,1)S(1)} collective-permute-done((bf16[1,128,128]{2,1,0:T(8,128)(2,1)S(1)}, bf16[1,128,128]{2,1,0:T(8,128)(2,1)S(1)}, u32[]{:S(2)}, u32[]{:S(2)}) %collective-permute-start.13) | collective-permute-done | bytes 32800 | tf_op jit(solution)/shard_map/ppermute | solution.py:18
  187.7 62.3 %all-reduce.25 = (f32[1]{0:T(128)}, f32[128]{0:T(128)}, f32[128]{0:T(128)}, f32[7,7,2,128]{3,2,1,0:T(2,128)}, f32[128]{0:T(128)}, /*index=5*/f32[128]{0:T(128)}, f32[128,2]{0,1:T(2,128)}, f32[2]{0:T(128)}) all-reduce(f32[1]{0:T(128)} %bitcast.60, ...), channel_id=1, replica_groups=mesh['groups'=2,'tm'=4,'space'=4] {'tm','space'}, use_global_device_ids=true, to_apply=%region_1.2 | all-reduce | flops 13315 | bytes 106520 | tf_op jit(solution)/shard_map/psum | solution.py:210
  250.0 39.9 %all-reduce.29.cloned.1.call-done = (f32[162,128]{1,0:T(8,128)}, f32[3,3,128,128]{3,2,1,0:T(8,128)}, f32[3,3,256,128]{3,2,1,0:T(8,128)}) async-done(((f32[162,128]{1,0:T(8,128)}, f32[3,3,128,128]{3,2,1,0:T(8,128)}, f32[3,3,256,128]{3,2,1,0:T(8,128)}), (f32[162,128]{1,0:T(8,128)}, f32[3,3,128,128]{3,2,1,0:T(8,128)}, f32[3,3,256,128]{3,2,1,0:T(8,128)})) %all-reduce.29.cloned.1.call-update) | async-done | bytes 1852432 | tf_op jit(solution)/shard_map/psum | solution.py:210
  289.9 1.6 copy.329
  291.5 1.9 copy.330
  (405 shorter events, 118.6 us)
Async XLA Ops:
  7.2 105.9 %copy-start = (bf16[162,128]{1,0:T(8,128)(2,1)S(1)}, bf16[162,128]{1,0:T(8,128)(2,1)}, u32[]{:S(2)}) copy-start(bf16[162,128]{1,0:T(8,128)(2,1)} %param.18) | copy-start | bytes 124420
  7.2 16.8 %copy-start.5 = (bf16[3,3,256,128]{3,2,1,0:T(8,128)(2,1)S(1)}, bf16[3,3,256,128]{3,2,1,0:T(8,128)(2,1)}, u32[]{:S(2)}) copy-start(bf16[3,3,256,128]{3,2,1,0:T(8,128)(2,1)} %param.24) | copy-start | bytes 1769476
  7.2 17.6 %copy-start.8 = (bf16[3,3,128,128]{3,2,1,0:T(8,128)(2,1)S(1)}, bf16[3,3,128,128]{3,2,1,0:T(8,128)(2,1)}, u32[]{:S(2)}) copy-start(bf16[3,3,128,128]{3,2,1,0:T(8,128)(2,1)} %param.20) | copy-start | bytes 884740
  7.2 282.6 %all-reduce.29.cloned.1.call-start = ((), (), s32[]{:S(2)}) async-start(), calls=%async_computation | async-start | bytes 3710976 | tf_op jit(solution)/shard_map/psum | solution.py:210
  8.4 20.4 %collective-permute-start = (bf16[4,128,256]{2,1,0:T(8,128)(2,1)S(1)}, bf16[4,128,256]{2,1,0:T(8,128)(2,1)S(1)}, u32[]{:S(2)}, u32[]{:S(2)}) collective-permute-start(bf16[4,128,256]{2,1,0:T(8,128)(2,1)S(1)} %get-tuple-element.61), channel_id=1, source_target_pairs={{0,1},{1,2},{2,3},{4,5},{5,6},{6,7},{8,9},{9,10},{10,11},{12,13},{... | collective-permute-start | bytes 786440 | tf_op jit(solution)/shard_map/ppermute | solution.py:17
  13.4 15.5 %collective-permute-start.1 = (bf16[4,128,256]{2,1,0:T(8,128)(2,1)S(1)}, bf16[4,128,256]{2,1,0:T(8,128)(2,1)S(1)}, u32[]{:S(2)}, u32[]{:S(2)}) collective-permute-start(bf16[4,128,256]{2,1,0:T(8,128)(2,1)S(1)} %get-tuple-element.62), channel_id=1, source_target_pairs={{1,0},{2,1},{3,2},{5,4},{6,5},{7,6},{9,8},{10,9},{11,10},{13,12},{... | collective-permute-start | bytes 786440 | tf_op jit(solution)/shard_map/ppermute | solution.py:18
  15.4 12.1 %collective-permute-start.6 = (bf16[2,3,128]{2,1,0:T(4,128)(2,1)S(1)}, bf16[2,3,128]{2,1,0:T(4,128)(2,1)S(1)}, u32[]{:S(2)}, u32[]{:S(2)}) collective-permute-start(bf16[2,3,128]{2,1,0:T(4,128)(2,1)S(1)} %get-tuple-element.186), channel_id=1, source_target_pairs={{0,1},{1,2},{2,3},{4,5},{5,6},{6,7},{8,9},{9,10},{10,11},{12,13},{... | collective-permute-start | bytes 4616 | tf_op jit(solution)/shard_map/ppermute | solution.py:17
  20.0 7.6 %collective-permute-start.7 = (bf16[2,3,128]{2,1,0:T(4,128)(2,1)S(1)}, bf16[2,3,128]{2,1,0:T(4,128)(2,1)S(1)}, u32[]{:S(2)}, u32[]{:S(2)}) collective-permute-start(bf16[2,3,128]{2,1,0:T(4,128)(2,1)S(1)} %get-tuple-element.187), channel_id=1, source_target_pairs={{1,0},{2,1},{3,2},{5,4},{6,5},{7,6},{9,8},{10,9},{11,10},{13,12},{... | collective-permute-start | bytes 4616 | tf_op jit(solution)/shard_map/ppermute | solution.py:18
  22.0 4.2 %copy-start.51 = (s32[1,2,8,128]{3,2,1,0:T(8,128)S(1)}, s32[1,2,8,128]{3,2,1,0:T(8,128)}, u32[]{:S(2)}) copy-start(s32[1,2,8,128]{3,2,1,0:T(8,128)} %param.17) | copy-start | bytes 24580
  22.0 4.9 %copy-start.50 = (bf16[7,7,2,128]{3,2,1,0:T(2,128)(2,1)S(1)}, bf16[7,7,2,128]{3,2,1,0:T(2,128)(2,1)}, u32[]{:S(2)}) copy-start(bf16[7,7,2,128]{3,2,1,0:T(2,128)(2,1)} %param.22) | copy-start | bytes 75268
  22.0 5.6 %copy-start.44 = (bf16[1,2,8,128]{3,2,1,0:T(8,128)(2,1)S(1)}, bf16[1,2,8,128]{3,2,1,0:T(8,128)(2,1)}, u32[]{:S(2)}) copy-start(bf16[1,2,8,128]{3,2,1,0:T(8,128)(2,1)} %param.16) | copy-start | bytes 12292
  24.0 4.9 %copy-start.6 = (bf16[1,8,128,256]{3,2,1,0:T(8,128)(2,1)S(1)}, bf16[1,8,128,256]{3,2,1,0:T(8,128)(2,1)}, u32[]{:S(2)}) copy-start(bf16[1,8,128,256]{3,2,1,0:T(8,128)(2,1)} %param.14) | copy-start | bytes 1572868
  29.9 6.5 %collective-permute-start.3 = (bf16[16,128,256]{2,1,0:T(8,128)(2,1)}, bf16[16,128,256]{2,1,0:T(8,128)(2,1)S(1)}, u32[]{:S(2)}, u32[]{:S(2)}) collective-permute-start(bf16[16,128,256]{2,1,0:T(8,128)(2,1)} %pad_maximum_fusion.2), channel_id=1, source_target_pairs={{4,0},{8,4},{12,8},{5,1},{9,5},{13,9},{6,2},{10,6},{14,10},{7,3},{... | collective-permute-start | bytes 3145736 | tf_op jit(solution)/shard_map/ppermute | solution.py:26
  32.2 37.7 %collective-permute-start.2 = (bf16[16,128,256]{2,1,0:T(8,128)(2,1)}, bf16[16,128,256]{2,1,0:T(8,128)(2,1)}, u32[]{:S(2)}, u32[]{:S(2)}) collective-permute-start(bf16[16,128,256]{2,1,0:T(8,128)(2,1)} %pad_maximum_fusion.2), channel_id=1, source_target_pairs={{0,4},{4,8},{8,12},{1,5},{5,9},{9,13},{2,6},{6,10},{10,14},{3,7},{... | collective-permute-start | bytes 3145736 | tf_op jit(solution)/shard_map/ppermute | solution.py:26
  113.1 7.1 %copy-start.49 = (bf16[98,128]{1,0:T(8,128)(2,1)S(1)}, bf16[98,128]{1,0:T(8,128)(2,1)}, u32[]{:S(2)}) copy-start(bf16[98,128]{1,0:T(8,128)(2,1)} %reshape.316) | copy-start | bytes 75268
  113.1 7.1 %copy-start.54 = (f32[128]{0:T(128)S(1)}, f32[128]{0:T(128)}, u32[]{:S(2)}) copy-start(f32[128]{0:T(128)} %param.23) | copy-start | bytes 1540
  114.4 7.0 %collective-permute-start.4 = (bf16[1,128,128]{2,1,0:T(8,128)(2,1)S(1)}, bf16[1,128,128]{2,1,0:T(8,128)(2,1)S(1)}, u32[]{:S(2)}, u32[]{:S(2)}) collective-permute-start(bf16[1,128,128]{2,1,0:T(8,128)(2,1)S(1)} %get-tuple-element.85), channel_id=1, source_target_pairs={{0,1},{1,2},{2,3},{4,5},{5,6},{6,7},{8,9},{9,10},{10,11},{12,13},{... | collective-permute-start | bytes 98312 | tf_op jit(solution)/shard_map/ppermute | solution.py:17
  118.9 5.8 %collective-permute-start.5 = (bf16[1,128,128]{2,1,0:T(8,128)(2,1)S(1)}, bf16[1,128,128]{2,1,0:T(8,128)(2,1)S(1)}, u32[]{:S(2)}, u32[]{:S(2)}) collective-permute-start(bf16[1,128,128]{2,1,0:T(8,128)(2,1)S(1)} %get-tuple-element.86), channel_id=1, source_target_pairs={{1,0},{2,1},{3,2},{5,4},{6,5},{7,6},{9,8},{10,9},{11,10},{13,12},{... | collective-permute-start | bytes 98312 | tf_op jit(solution)/shard_map/ppermute | solution.py:18
  132.0 5.4 %collective-permute-start.8 = (bf16[1,128,256]{2,1,0:T(8,128)(2,1)S(1)}, bf16[1,128,256]{2,1,0:T(8,128)(2,1)S(1)}, u32[]{:S(2)}, u32[]{:S(2)}) collective-permute-start(bf16[1,128,256]{2,1,0:T(8,128)(2,1)S(1)} %get-tuple-element.59), channel_id=1, source_target_pairs={{0,1},{1,2},{2,3},{4,5},{5,6},{6,7},{8,9},{9,10},{10,11},{12,13},{... | collective-permute-start | bytes 196616 | tf_op jit(solution)/shard_map/ppermute | solution.py:17
  135.5 6.2 %collective-permute-start.9 = (bf16[1,128,256]{2,1,0:T(8,128)(2,1)S(1)}, bf16[1,128,256]{2,1,0:T(8,128)(2,1)S(1)}, u32[]{:S(2)}, u32[]{:S(2)}) collective-permute-start(bf16[1,128,256]{2,1,0:T(8,128)(2,1)S(1)} %get-tuple-element.60), channel_id=1, source_target_pairs={{1,0},{2,1},{3,2},{5,4},{6,5},{7,6},{9,8},{10,9},{11,10},{13,12},{... | collective-permute-start | bytes 196616 | tf_op jit(solution)/shard_map/ppermute | solution.py:18
  159.1 5.9 %collective-permute-start.10 = (bf16[1,128,128]{2,1,0:T(8,128)(2,1)S(1)}, bf16[1,128,128]{2,1,0:T(8,128)(2,1)S(1)}, u32[]{:S(2)}, u32[]{:S(2)}) collective-permute-start(bf16[1,128,128]{2,1,0:T(8,128)(2,1)S(1)} %get-tuple-element.83), channel_id=1, source_target_pairs={{0,1},{1,2},{2,3},{4,5},{5,6},{6,7},{8,9},{9,10},{10,11},{12,13},{... | collective-permute-start | bytes 98312 | tf_op jit(solution)/shard_map/ppermute | solution.py:17
  162.6 5.8 %collective-permute-start.11 = (bf16[1,128,128]{2,1,0:T(8,128)(2,1)S(1)}, bf16[1,128,128]{2,1,0:T(8,128)(2,1)S(1)}, u32[]{:S(2)}, u32[]{:S(2)}) collective-permute-start(bf16[1,128,128]{2,1,0:T(8,128)(2,1)S(1)} %get-tuple-element.84), channel_id=1, source_target_pairs={{1,0},{2,1},{3,2},{5,4},{6,5},{7,6},{9,8},{10,9},{11,10},{13,12},{... | collective-permute-start | bytes 98312 | tf_op jit(solution)/shard_map/ppermute | solution.py:18
  174.0 4.1 %collective-permute-start.12 = (bf16[1,128,128]{2,1,0:T(8,128)(2,1)S(1)}, bf16[1,128,128]{2,1,0:T(8,128)(2,1)S(1)}, u32[]{:S(2)}, u32[]{:S(2)}) collective-permute-start(bf16[1,128,128]{2,1,0:T(8,128)(2,1)S(1)} %get-tuple-element.81), channel_id=1, source_target_pairs={{0,1},{1,2},{2,3},{4,5},{5,6},{6,7},{8,9},{9,10},{10,11},{12,13},{... | collective-permute-start | bytes 98312 | tf_op jit(solution)/shard_map/ppermute | solution.py:17
  176.0 5.8 %collective-permute-start.13 = (bf16[1,128,128]{2,1,0:T(8,128)(2,1)S(1)}, bf16[1,128,128]{2,1,0:T(8,128)(2,1)S(1)}, u32[]{:S(2)}, u32[]{:S(2)}) collective-permute-start(bf16[1,128,128]{2,1,0:T(8,128)(2,1)S(1)} %get-tuple-element.82), channel_id=1, source_target_pairs={{1,0},{2,1},{3,2},{5,4},{6,5},{7,6},{9,8},{10,9},{11,10},{13,12},{... | collective-permute-start | bytes 98312 | tf_op jit(solution)/shard_map/ppermute | solution.py:18
  (51 other events, 63.6 us)
Sparse Core Ops, SparseCore 0:
  186.1 103.6 all-reduce.28
where the time goes:
time: 306 us; the launch traced here: 302 us
  local copies, waits for them, and re-layouts  80 us (26%)
  blocking collectives  62.3 us (20%)
  waiting for transfers between devices  54.9 us (18%)
  matrix products  45.1 us (15%)
  starting transfers between devices  36.4 us (12%)
  between operations  18.2 us (6%)
  other arithmetic  4.82 us (2%)
    psum x1, blocking collectives, local(): lax.psum((loss_local, grad_w_volume, grad_b_volume, grad_w_code, grad_b_c...  62.3 us
    psum x1, waiting for transfers between devices, local(): lax.psum((loss_local, grad_w_volume, grad_b_volume, grad_w_code, grad_b_c...  39.9 us
    dot_general x18, matrix products, correlate(): jnp.einsum('rxc,ryc->rxy', own_tile, window, preferred_element_type=jnp.f...  24.8 us
    ppermute x6, starting transfers between devices, extended_2(): before = lax.ppermute(last, axis, up)  22.9 us
    reshape x18, local copies, waits for them, and re-layouts, correlate(): flat_scores.reshape(n_rows, n_cols, n_cols + side)[:, :, :side]  20.9 us
    ppermute x6, waiting for transfers between devices, extended_2(): after = lax.ppermute(first, axis, down)  14.7 us
    unnamed x150, local copies, waits for them, and re-layouts  12.4 us
    another operation x37, local copies, waits for them, and re-layouts, correlate(): stacked = jnp.stack(bands, axis=2).reshape(n_rows, n_cols, side * side)  10.8 us
  transfers between devices with their start and end apart: 15, of which 6 were waited for; matrix products, arithmetic and copies ran while one was open for 15% of the time, Pallas kernels for 0%

commit v1 on v0

--- a/solution.py
+++ b/solution.py
@@ -208,20 +208,23 @@
         grad_w_head,
         grad_b_head,
     ) = lax.psum(
-        (
-            loss_local,
-            grad_w_volume,
-            grad_b_volume,
-            grad_w_code,
-            grad_b_code,
-            grad_w_flow,
-            grad_b_flow,
-            grad_w_joint,
-            grad_b_joint,
-            grad_w_head,
-            grad_b_head,
+        lax.psum(
+            (
+                loss_local,
+                grad_w_volume,
+                grad_b_volume,
+                grad_w_code,
+                grad_b_code,
+                grad_w_flow,
+                grad_b_flow,
+                grad_w_joint,
+                grad_b_joint,
+                grad_w_head,
+                grad_b_head,
+            ),
+            "space",
         ),
-        ("tm", "space"),
+        "tm",
     )
     return (
         loss_local,

time: 306 us -> 338 us (1.10)
  waiting for transfers between devices: 54.9 us -> 118 us
  blocking collectives: 62.3 us -> 30.9 us
    psum x1, waiting for transfers between devices: 39.9 us -> 85.7 us  [local(): lax.psum((loss_local, grad_w_volume, grad_b_volume, grad_w_code, grad_b_c...]
    psum x1, blocking collectives: 62.3 us -> 19.2 us  [local(): lax.psum((loss_local, grad_w_volume, grad_b_volume, grad_w_code, grad_b_c...]
    psum x0 -> x1, waiting for transfers between devices: none -> 17.2 us  [local(): lax.psum(lax.psum((loss_local, grad_w_volume, grad_b_volume, grad_w_code,...]
    psum x0 -> x1, blocking collectives: none -> 11.7 us  [local(): lax.psum(lax.psum((loss_local, grad_w_volume, grad_b_volume, grad_w_code,...]
  transfers between devices with their start and end apart: 15 -> 16, of which waited for: 6 -> 7; matrix products, arithmetic and copies ran while one was open for 15% -> 13% of each run, Pallas kernels for 0% -> 0%
where the time goes in v1:
time: 338 us; the launch traced here: 333 us
  waiting for transfers between devices  118 us (35%)
  local copies, waits for them, and re-layouts  80.1 us (24%)
  matrix products  45.1 us (13%)
  starting transfers between devices  36.5 us (11%)
  blocking collectives  30.9 us (9%)
  between operations  18.2 us (5%)
  other arithmetic  4.82 us (1%)
    psum x1, waiting for transfers between devices, local(): lax.psum((loss_local, grad_w_volume, grad_b_volume, grad_w_code, grad_b_c...  85.7 us
    dot_general x18, matrix products, correlate(): jnp.einsum('rxc,ryc->rxy', own_tile, window, preferred_element_type=jnp.f...  24.8 us
    ppermute x6, starting transfers between devices, extended_2(): before = lax.ppermute(last, axis, up)  22.9 us
    reshape x18, local copies, waits for them, and re-layouts, correlate(): flat_scores.reshape(n_rows, n_cols, n_cols + side)[:, :, :side]  20.9 us
    psum x1, blocking collectives, local(): lax.psum((loss_local, grad_w_volume, grad_b_volume, grad_w_code, grad_b_c...  19.2 us
    psum x1, waiting for transfers between devices, local(): lax.psum(lax.psum((loss_local, grad_w_volume, grad_b_volume, grad_w_code,...  17.2 us
    ppermute x6, waiting for transfers between devices, extended_2(): after = lax.ppermute(first, axis, down)  14.7 us
    unnamed x150, local copies, waits for them, and re-layouts  12.4 us
  transfers between devices with their start and end apart: 16, of which 7 were waited for; matrix products, arithmetic and copies ran while one was open for 13% of the time, Pallas kernels for 0%

profile of v1, /device:TPU:0, one launch (start us, length us, event | category | flops | bytes accessed | tf_op | source)
XLA Modules:
  0.0 333.5 jit_solution(13241918496857038073)
XLA Ops:
  8.4 4.9 %collective-permute-start = (bf16[4,128,256]{2,1,0:T(8,128)(2,1)S(1)}, bf16[4,128,256]{2,1,0:T(8,128)(2,1)S(1)}, u32[]{:S(2)}, u32[]{:S(2)}) collective-permute-start(bf16[4,128,256]{2,1,0:T(8,128)(2,1)S(1)} %get-tuple-element.72), channel_id=1, source_target_pairs={{0,1},{1,2},{2,3},{4,5},{5,6},{6,7},{8,9},{9,10},{10,11},{12,13},{... | collective-permute-start | bytes 786440 | tf_op jit(solution)/shard_map/ppermute | solution.py:17
  15.4 4.5 %collective-permute-start.6 = (bf16[2,3,128]{2,1,0:T(4,128)(2,1)S(1)}, bf16[2,3,128]{2,1,0:T(4,128)(2,1)S(1)}, u32[]{:S(2)}, u32[]{:S(2)}) collective-permute-start(bf16[2,3,128]{2,1,0:T(4,128)(2,1)S(1)} %get-tuple-element.197), channel_id=1, source_target_pairs={{0,1},{1,2},{2,3},{4,5},{5,6},{6,7},{8,9},{9,10},{10,11},{12,13},{... | collective-permute-start | bytes 4616 | tf_op jit(solution)/shard_map/ppermute | solution.py:17
  22.0 2.0 fusion.158
  32.2 4.2 %collective-permute-start.2 = (bf16[16,128,256]{2,1,0:T(8,128)(2,1)}, bf16[16,128,256]{2,1,0:T(8,128)(2,1)}, u32[]{:S(2)}, u32[]{:S(2)}) collective-permute-start(bf16[16,128,256]{2,1,0:T(8,128)(2,1)} %pad_maximum_fusion.2), channel_id=1, source_target_pairs={{0,4},{4,8},{8,12},{1,5},{5,9},{9,13},{2,6},{6,10},{10,14},{3,7},{... | collective-permute-start | bytes 3145736 | tf_op jit(solution)/shard_map/ppermute | solution.py:26
  55.9 1.8 convolution_bitcast_fusion.3
  114.4 4.5 %collective-permute-start.4 = (bf16[1,128,128]{2,1,0:T(8,128)(2,1)S(1)}, bf16[1,128,128]{2,1,0:T(8,128)(2,1)S(1)}, u32[]{:S(2)}, u32[]{:S(2)}) collective-permute-start(bf16[1,128,128]{2,1,0:T(8,128)(2,1)S(1)} %get-tuple-element.96), channel_id=1, source_target_pairs={{0,1},{1,2},{2,3},{4,5},{5,6},{6,7},{8,9},{9,10},{10,11},{12,13},{... | collective-permute-start | bytes 98312 | tf_op jit(solution)/shard_map/ppermute | solution.py:17
  121.3 3.4 %collective-permute-done.5 = bf16[1,128,128]{2,1,0:T(8,128)(2,1)S(1)} collective-permute-done((bf16[1,128,128]{2,1,0:T(8,128)(2,1)S(1)}, bf16[1,128,128]{2,1,0:T(8,128)(2,1)S(1)}, u32[]{:S(2)}, u32[]{:S(2)}) %collective-permute-start.5) | collective-permute-done | bytes 32800 | tf_op jit(solution)/shard_map/ppermute | solution.py:18
  132.0 3.5 %collective-permute-start.8 = (bf16[1,128,256]{2,1,0:T(8,128)(2,1)S(1)}, bf16[1,128,256]{2,1,0:T(8,128)(2,1)S(1)}, u32[]{:S(2)}, u32[]{:S(2)}) collective-permute-start(bf16[1,128,256]{2,1,0:T(8,128)(2,1)S(1)} %get-tuple-element.70), channel_id=1, source_target_pairs={{0,1},{1,2},{2,3},{4,5},{5,6},{6,7},{8,9},{9,10},{10,11},{12,13},{... | collective-permute-start | bytes 196616 | tf_op jit(solution)/shard_map/ppermute | solution.py:17
  137.4 4.3 %collective-permute-done.9 = bf16[1,128,256]{2,1,0:T(8,128)(2,1)S(1)} collective-permute-done((bf16[1,128,256]{2,1,0:T(8,128)(2,1)S(1)}, bf16[1,128,256]{2,1,0:T(8,128)(2,1)S(1)}, u32[]{:S(2)}, u32[]{:S(2)}) %collective-permute-start.9) | collective-permute-done | bytes 65568 | tf_op jit(solution)/shard_map/ppermute | solution.py:18
  142.2 1.7 fusion.153
  143.9 1.6 copy.98
  145.5 2.4 fusion.165
  148.7 2.3 fusion.166
  151.0 1.7 copy.97
  152.7 2.4 multiply_convert_fusion
  159.1 3.5 %collective-permute-start.10 = (bf16[1,128,128]{2,1,0:T(8,128)(2,1)S(1)}, bf16[1,128,128]{2,1,0:T(8,128)(2,1)S(1)}, u32[]{:S(2)}, u32[]{:S(2)}) collective-permute-start(bf16[1,128,128]{2,1,0:T(8,128)(2,1)S(1)} %get-tuple-element.94), channel_id=1, source_target_pairs={{0,1},{1,2},{2,3},{4,5},{5,6},{6,7},{8,9},{9,10},{10,11},{12,13},{... | collective-permute-start | bytes 98312 | tf_op jit(solution)/shard_map/ppermute | solution.py:17
  165.0 3.4 %collective-permute-done.11 = bf16[1,128,128]{2,1,0:T(8,128)(2,1)S(1)} collective-permute-done((bf16[1,128,128]{2,1,0:T(8,128)(2,1)S(1)}, bf16[1,128,128]{2,1,0:T(8,128)(2,1)S(1)}, u32[]{:S(2)}, u32[]{:S(2)}) %collective-permute-start.11) | collective-permute-done | bytes 32800 | tf_op jit(solution)/shard_map/ppermute | solution.py:18
  174.0 1.9 collective-permute-start.12
  178.1 3.6 %collective-permute-done.13 = bf16[1,128,128]{2,1,0:T(8,128)(2,1)S(1)} collective-permute-done((bf16[1,128,128]{2,1,0:T(8,128)(2,1)S(1)}, bf16[1,128,128]{2,1,0:T(8,128)(2,1)S(1)}, u32[]{:S(2)}, u32[]{:S(2)}) %collective-permute-start.13) | collective-permute-done | bytes 32800 | tf_op jit(solution)/shard_map/ppermute | solution.py:18
  186.0 85.7 %all-reduce.32.cloned.1.call-done = (f32[162,128]{1,0:T(8,128)}, f32[3,3,128,128]{3,2,1,0:T(8,128)}, f32[3,3,256,128]{3,2,1,0:T(8,128)}) async-done(((f32[162,128]{1,0:T(8,128)}, f32[3,3,128,128]{3,2,1,0:T(8,128)}, f32[3,3,256,128]{3,2,1,0:T(8,128)}), (f32[162,128]{1,0:T(8,128)}, f32[3,3,128,128]{3,2,1,0:T(8,128)}, f32[3,3,256,128]{3,2,1,0:T(8,128)})) %all-reduce.32.cloned.1.call-update) | async-done | bytes 1852432 | tf_op jit(solution)/shard_map/psum | solution.py:211
  273.5 19.2 %all-reduce.25 = (f32[1]{0:T(128)}, f32[128]{0:T(128)S(1)}, f32[128]{0:T(128)S(1)}, f32[7,7,2,128]{3,2,1,0:T(2,128)S(1)}, f32[128]{0:T(128)S(1)}, /*index=5*/f32...) all-reduce(f32[1]{0:T(128)} %bitcast.60, ...), channel_id=1, replica_groups=mesh['groups'=2,'tm'=4,'space'=4] {'space'}, use_global_device_ids=true, to_apply=%region_1.2 | all-reduce | flops 13315 | bytes 106520 | tf_op jit(solution)/shard_map/psum | solution.py:211
  292.7 11.7 %all-reduce.27 = (f32[1]{0:T(128)}, f32[128]{0:T(128)}, f32[128]{0:T(128)}, f32[7,7,2,128]{3,2,1,0:T(2,128)}, f32[128]{0:T(128)}, /*index=5*/f32[128]{0:T(128)}, f32[128,2]{0,1:T(2,128)}, f32[2]{0:T(128)}) all-reduce(f32[1]{0:T(128)} %get-tuple-element.12, ...), channel_id=1, replica_groups=mesh['groups'=2,'tm'=4,'space'=4] {'tm'}, use_global_device_ids=true, to_apply=%region_2.3 | all-reduce | flops 13315 | bytes 106520 | tf_op jit(solution)/shard_map/psum | solution.py:210
  304.4 17.2 %all-reduce.34.cloned.1.call-done = (f32[162,128]{1,0:T(8,128)}, f32[3,3,128,128]{3,2,1,0:T(8,128)}, f32[3,3,256,128]{3,2,1,0:T(8,128)}) async-done(((f32[162,128]{1,0:T(8,128)}, f32[3,3,128,128]{3,2,1,0:T(8,128)}, f32[3,3,256,128]{3,2,1,0:T(8,128)}), (f32[162,128]{1,0:T(8,128)}, f32[3,3,128,128]{3,2,1,0:T(8,128)}, f32[3,3,256,128]{3,2,1,0:T(8,128)})) %all-reduce.34.cloned.1.call-update) | async-done | bytes 1852432 | tf_op jit(solution)/shard_map/psum | solution.py:210
  323.3 1.9 copy.333
  (409 shorter events, 121.9 us)
Async XLA Ops:
  7.2 105.9 %copy-start = (bf16[162,128]{1,0:T(8,128)(2,1)S(1)}, bf16[162,128]{1,0:T(8,128)(2,1)}, u32[]{:S(2)}) copy-start(bf16[162,128]{1,0:T(8,128)(2,1)} %param.18) | copy-start | bytes 124420
  7.2 16.8 %copy-start.5 = (bf16[3,3,256,128]{3,2,1,0:T(8,128)(2,1)S(1)}, bf16[3,3,256,128]{3,2,1,0:T(8,128)(2,1)}, u32[]{:S(2)}) copy-start(bf16[3,3,256,128]{3,2,1,0:T(8,128)(2,1)} %param.24) | copy-start | bytes 1769476
  7.2 17.6 %copy-start.8 = (bf16[3,3,128,128]{3,2,1,0:T(8,128)(2,1)S(1)}, bf16[3,3,128,128]{3,2,1,0:T(8,128)(2,1)}, u32[]{:S(2)}) copy-start(bf16[3,3,128,128]{3,2,1,0:T(8,128)(2,1)} %param.20) | copy-start | bytes 884740
  7.2 264.5 %all-reduce.32.cloned.1.call-start = ((), (), s32[]{:S(2)}) async-start(), calls=%async_computation | async-start | bytes 3710976 | tf_op jit(solution)/shard_map/psum | solution.py:211
  8.4 20.4 %collective-permute-start = (bf16[4,128,256]{2,1,0:T(8,128)(2,1)S(1)}, bf16[4,128,256]{2,1,0:T(8,128)(2,1)S(1)}, u32[]{:S(2)}, u32[]{:S(2)}) collective-permute-start(bf16[4,128,256]{2,1,0:T(8,128)(2,1)S(1)} %get-tuple-element.72), channel_id=1, source_target_pairs={{0,1},{1,2},{2,3},{4,5},{5,6},{6,7},{8,9},{9,10},{10,11},{12,13},{... | collective-permute-start | bytes 786440 | tf_op jit(solution)/shard_map/ppermute | solution.py:17
  13.4 15.5 %collective-permute-start.1 = (bf16[4,128,256]{2,1,0:T(8,128)(2,1)S(1)}, bf16[4,128,256]{2,1,0:T(8,128)(2,1)S(1)}, u32[]{:S(2)}, u32[]{:S(2)}) collective-permute-start(bf16[4,128,256]{2,1,0:T(8,128)(2,1)S(1)} %get-tuple-element.73), channel_id=1, source_target_pairs={{1,0},{2,1},{3,2},{5,4},{6,5},{7,6},{9,8},{10,9},{11,10},{13,12},{... | collective-permute-start | bytes 786440 | tf_op jit(solution)/shard_map/ppermute | solution.py:18
  15.4 12.1 %collective-permute-start.6 = (bf16[2,3,128]{2,1,0:T(4,128)(2,1)S(1)}, bf16[2,3,128]{2,1,0:T(4,128)(2,1)S(1)}, u32[]{:S(2)}, u32[]{:S(2)}) collective-permute-start(bf16[2,3,128]{2,1,0:T(4,128)(2,1)S(1)} %get-tuple-element.197), channel_id=1, source_target_pairs={{0,1},{1,2},{2,3},{4,5},{5,6},{6,7},{8,9},{9,10},{10,11},{12,13},{... | collective-permute-start | bytes 4616 | tf_op jit(solution)/shard_map/ppermute | solution.py:17
  20.0 7.6 %collective-permute-start.7 = (bf16[2,3,128]{2,1,0:T(4,128)(2,1)S(1)}, bf16[2,3,128]{2,1,0:T(4,128)(2,1)S(1)}, u32[]{:S(2)}, u32[]{:S(2)}) collective-permute-start(bf16[2,3,128]{2,1,0:T(4,128)(2,1)S(1)} %get-tuple-element.198), channel_id=1, source_target_pairs={{1,0},{2,1},{3,2},{5,4},{6,5},{7,6},{9,8},{10,9},{11,10},{13,12},{... | collective-permute-start | bytes 4616 | tf_op jit(solution)/shard_map/ppermute | solution.py:18
  22.0 4.9 %copy-start.50 = (bf16[7,7,2,128]{3,2,1,0:T(2,128)(2,1)S(1)}, bf16[7,7,2,128]{3,2,1,0:T(2,128)(2,1)}, u32[]{:S(2)}) copy-start(bf16[7,7,2,128]{3,2,1,0:T(2,128)(2,1)} %param.22) | copy-start | bytes 75268
  22.0 5.6 %copy-start.44 = (bf16[1,2,8,128]{3,2,1,0:T(8,128)(2,1)S(1)}, bf16[1,2,8,128]{3,2,1,0:T(8,128)(2,1)}, u32[]{:S(2)}) copy-start(bf16[1,2,8,128]{3,2,1,0:T(8,128)(2,1)} %param.16) | copy-start | bytes 12292
  29.9 6.5 %collective-permute-start.3 = (bf16[16,128,256]{2,1,0:T(8,128)(2,1)}, bf16[16,128,256]{2,1,0:T(8,128)(2,1)S(1)}, u32[]{:S(2)}, u32[]{:S(2)}) collective-permute-start(bf16[16,128,256]{2,1,0:T(8,128)(2,1)} %pad_maximum_fusion.2), channel_id=1, source_target_pairs={{4,0},{8,4},{12,8},{5,1},{9,5},{13,9},{6,2},{10,6},{14,10},{7,3},{... | collective-permute-start | bytes 3145736 | tf_op jit(solution)/shard_map/ppermute | solution.py:26
  32.2 37.7 %collective-permute-start.2 = (bf16[16,128,256]{2,1,0:T(8,128)(2,1)}, bf16[16,128,256]{2,1,0:T(8,128)(2,1)}, u32[]{:S(2)}, u32[]{:S(2)}) collective-permute-start(bf16[16,128,256]{2,1,0:T(8,128)(2,1)} %pad_maximum_fusion.2), channel_id=1, source_target_pairs={{0,4},{4,8},{8,12},{1,5},{5,9},{9,13},{2,6},{6,10},{10,14},{3,7},{... | collective-permute-start | bytes 3145736 | tf_op jit(solution)/shard_map/ppermute | solution.py:26
  113.1 7.1 %copy-start.49 = (bf16[98,128]{1,0:T(8,128)(2,1)S(1)}, bf16[98,128]{1,0:T(8,128)(2,1)}, u32[]{:S(2)}) copy-start(bf16[98,128]{1,0:T(8,128)(2,1)} %reshape.316) | copy-start | bytes 75268
  113.1 7.1 %copy-start.54 = (f32[128]{0:T(128)S(1)}, f32[128]{0:T(128)}, u32[]{:S(2)}) copy-start(f32[128]{0:T(128)} %param.23) | copy-start | bytes 1540
  114.4 7.0 %collective-permute-start.4 = (bf16[1,128,128]{2,1,0:T(8,128)(2,1)S(1)}, bf16[1,128,128]{2,1,0:T(8,128)(2,1)S(1)}, u32[]{:S(2)}, u32[]{:S(2)}) collective-permute-start(bf16[1,128,128]{2,1,0:T(8,128)(2,1)S(1)} %get-tuple-element.96), channel_id=1, source_target_pairs={{0,1},{1,2},{2,3},{4,5},{5,6},{6,7},{8,9},{9,10},{10,11},{12,13},{... | collective-permute-start | bytes 98312 | tf_op jit(solution)/shard_map/ppermute | solution.py:17
  118.9 5.8 %collective-permute-start.5 = (bf16[1,128,128]{2,1,0:T(8,128)(2,1)S(1)}, bf16[1,128,128]{2,1,0:T(8,128)(2,1)S(1)}, u32[]{:S(2)}, u32[]{:S(2)}) collective-permute-start(bf16[1,128,128]{2,1,0:T(8,128)(2,1)S(1)} %get-tuple-element.97), channel_id=1, source_target_pairs={{1,0},{2,1},{3,2},{5,4},{6,5},{7,6},{9,8},{10,9},{11,10},{13,12},{... | collective-permute-start | bytes 98312 | tf_op jit(solution)/shard_map/ppermute | solution.py:18
  132.0 5.4 %collective-permute-start.8 = (bf16[1,128,256]{2,1,0:T(8,128)(2,1)S(1)}, bf16[1,128,256]{2,1,0:T(8,128)(2,1)S(1)}, u32[]{:S(2)}, u32[]{:S(2)}) collective-permute-start(bf16[1,128,256]{2,1,0:T(8,128)(2,1)S(1)} %get-tuple-element.70), channel_id=1, source_target_pairs={{0,1},{1,2},{2,3},{4,5},{5,6},{6,7},{8,9},{9,10},{10,11},{12,13},{... | collective-permute-start | bytes 196616 | tf_op jit(solution)/shard_map/ppermute | solution.py:17
  135.5 6.2 %collective-permute-start.9 = (bf16[1,128,256]{2,1,0:T(8,128)(2,1)S(1)}, bf16[1,128,256]{2,1,0:T(8,128)(2,1)S(1)}, u32[]{:S(2)}, u32[]{:S(2)}) collective-permute-start(bf16[1,128,256]{2,1,0:T(8,128)(2,1)S(1)} %get-tuple-element.71), channel_id=1, source_target_pairs={{1,0},{2,1},{3,2},{5,4},{6,5},{7,6},{9,8},{10,9},{11,10},{13,12},{... | collective-permute-start | bytes 196616 | tf_op jit(solution)/shard_map/ppermute | solution.py:18
  159.1 5.9 %collective-permute-start.10 = (bf16[1,128,128]{2,1,0:T(8,128)(2,1)S(1)}, bf16[1,128,128]{2,1,0:T(8,128)(2,1)S(1)}, u32[]{:S(2)}, u32[]{:S(2)}) collective-permute-start(bf16[1,128,128]{2,1,0:T(8,128)(2,1)S(1)} %get-tuple-element.94), channel_id=1, source_target_pairs={{0,1},{1,2},{2,3},{4,5},{5,6},{6,7},{8,9},{9,10},{10,11},{12,13},{... | collective-permute-start | bytes 98312 | tf_op jit(solution)/shard_map/ppermute | solution.py:17
  162.6 5.8 %collective-permute-start.11 = (bf16[1,128,128]{2,1,0:T(8,128)(2,1)S(1)}, bf16[1,128,128]{2,1,0:T(8,128)(2,1)S(1)}, u32[]{:S(2)}, u32[]{:S(2)}) collective-permute-start(bf16[1,128,128]{2,1,0:T(8,128)(2,1)S(1)} %get-tuple-element.95), channel_id=1, source_target_pairs={{1,0},{2,1},{3,2},{5,4},{6,5},{7,6},{9,8},{10,9},{11,10},{13,12},{... | collective-permute-start | bytes 98312 | tf_op jit(solution)/shard_map/ppermute | solution.py:18
  174.0 4.1 %collective-permute-start.12 = (bf16[1,128,128]{2,1,0:T(8,128)(2,1)S(1)}, bf16[1,128,128]{2,1,0:T(8,128)(2,1)S(1)}, u32[]{:S(2)}, u32[]{:S(2)}) collective-permute-start(bf16[1,128,128]{2,1,0:T(8,128)(2,1)S(1)} %get-tuple-element.92), channel_id=1, source_target_pairs={{0,1},{1,2},{2,3},{4,5},{5,6},{6,7},{8,9},{9,10},{10,11},{12,13},{... | collective-permute-start | bytes 98312 | tf_op jit(solution)/shard_map/ppermute | solution.py:17
  176.0 5.8 %collective-permute-start.13 = (bf16[1,128,128]{2,1,0:T(8,128)(2,1)S(1)}, bf16[1,128,128]{2,1,0:T(8,128)(2,1)S(1)}, u32[]{:S(2)}, u32[]{:S(2)}) collective-permute-start(bf16[1,128,128]{2,1,0:T(8,128)(2,1)S(1)} %get-tuple-element.93), channel_id=1, source_target_pairs={{1,0},{2,1},{3,2},{5,4},{6,5},{7,6},{9,8},{10,9},{11,10},{13,12},{... | collective-permute-start | bytes 98312 | tf_op jit(solution)/shard_map/ppermute | solution.py:18
  186.0 87.1 %copy-start.22 = (bf16[1024,128]{1,0:T(8,128)(2,1)S(1)}, bf16[1024,128]{1,0:T(8,128)(2,1)}, u32[]{:S(2)}) copy-start(bf16[1024,128]{1,0:T(8,128)(2,1)} %copy-done.21) | copy-start | bytes 786436
  186.0 135.6 %all-reduce.34.cloned.1.call-start = ((), (), s32[]{:S(2)}) async-start(), calls=%async_computation.1 | async-start | bytes 3710976 | tf_op jit(solution)/shard_map/psum | solution.py:210
  (52 other events, 70.0 us)
Sparse Core Ops, SparseCore 0:
  186.1 85.5 all-reduce.31
  274.3 47.2 all-reduce.33
